TPU v7x, 32 devices: a whole 2x2x4 slice. The times are simulated.
32 devices in a mesh: clip: 2 (over y), tile: 4 (over z), slab: 2 (over x), chan: 2 (over core).
Axes of the slice: x: 2, y: 2, z: 4, core: 2. Of those that a mesh axis runs over, the one named last changes fastest.
Arguments:
- video: bfloat16 [16, 16, 128, 128], P(('clip', 'slab'), 'tile'), parts along dimension 0, may hold values from -6 to 6
- first_weight: bfloat16 [3, 3, 3, 128, 128], P(None, None, None, None, 'chan'), may hold values from -0.109375 to 0.109375
- first_bias: float32 [128], P('chan'), may hold values from -3 to 3
- second_weight: bfloat16 [3, 3, 3, 128, 256], replicated, may hold values from -0.109375 to 0.109375
- second_bias: float32 [256], P('chan'), may hold values from -3 to 3
Outputs:
- latents: bfloat16 [8, 16, 128, 256], P(('clip', 'slab'), 'tile', None, 'chan'), parts along dimension 0
There are 2 independent parts, one for each index of `clip`. A program takes and returns all parts, laid end to end along the dimension named above; an argument that names none is the same for every part. Nothing has to cross between parts.
All inputs are finite; a program needn't handle non-finite values.
Results may differ from a plain program's by a relative error of at most 0.0095.
Values may be sent and summed in bfloat16 or wider, within the bound.
A program may use at most 64 MiB of HBM per device.

v0:
```python
import functools

import jax
import jax.numpy as jnp
from jax import lax
from jax.experimental import pallas as pl
from jax.experimental.pallas import tpu as pltpu
from jax.sharding import PartitionSpec as P

MESH = pl.DeviceIdType.MESH
BACK = 2


def kernel(
    tiles, slabs, video, w1, b1, w2, b2, out,
    v, h, k1, k2, b1_peer, b2_peer, going,
    local_sem, w1_sem, w2_sem, h_send, h_recv, e_send, e_recv, q_send, q_recv, small_send, small_recv, own_send, own_recv,
    x_send, x_recv, z_send, z_recv, p_send, p_recv, o_send, o_recv,
):
    frames, rows, columns, channels = video.shape
    half = rows // 2
    core = lax.axis_index("chan")
    tile = lax.axis_index("tile")
    slab = lax.axis_index("slab")
    other = 1 - core
    z_tile = tile + 2 * core - 1
    has_z = jnp.logical_and(z_tile >= 0, z_tile < tiles)
    no_z = jnp.logical_or(z_tile < 0, z_tile >= tiles)
    has_next = slab < slabs - 1
    has_prev = slab > 0
    peer = {"chan": other}
    z_peer = {"chan": other, "tile": z_tile}
    following = {"slab": slab + 1}
    preceding = {"slab": slab - 1}

    def remote(src, dst, send, recv, device):
        return pltpu.make_async_remote_copy(
            src_ref=src, dst_ref=dst, send_sem=send, recv_sem=recv,
            device_id=device, device_id_type=MESH,
        )

    mine = pl.ds(half * core, half)
    halo_here = pl.ds(rows * core, half)
    halo_there = pl.ds(rows * other, half)
    inner_here = pl.ds(rows * other, half)
    inner_there = pl.ds(rows * core, half)
    arrived = pl.ds(half, half)

    into_v = pltpu.make_async_copy(
        video,
        v.at[pl.ds(BACK, frames), pl.ds(half * other, rows)],
        local_sem,
    )
    into_v.start()
    own_w1 = pltpu.make_async_copy(w1, k1.at[:, :, 0], w1_sem)
    own_w1.start()
    part = channels // 2
    width = b2.shape[1]
    w2_copies = []
    for e in range(3):
        for n in range(2):
            for k in range(2):
                owner_n = core if n == 0 else other
                owner_k = core if k == 0 else other
                w2_copies.append(
                    pltpu.make_async_copy(
                        w2.at[:, e, pl.ds(pl.multiple_of(owner_k * part, part), part),
                              pl.ds(pl.multiple_of(owner_n * width, width), width)],
                        k2.at[:, pl.ds(k * part, part), pl.ds((2 * e + n) * width, width)],
                        w2_sem.at[len(w2_copies)],
                    )
                )
    barrier = pltpu.get_barrier_semaphore()
    everyone = ((None, peer), (has_z, z_peer), (has_next, following), (has_prev, preceding))

    def when(condition, body):
        if condition is None:
            body()
        else:
            pl.when(condition)(body)

    for condition, device in everyone:
        when(condition, lambda device=device: pl.semaphore_signal(
            barrier, inc=1, device_id=device, device_id_type=MESH))
    into_v.wait()
    own_w1.wait()
    met = 1 + sum(jnp.where(condition, 1, 0) for condition, _ in everyone[1:])
    pl.semaphore_wait(barrier, met)

    small = [
        remote(k1.at[:, :, 0], k1.at[:, :, 1], small_send.at[0], small_recv.at[0], peer),
        remote(b1, b1_peer, small_send.at[1], small_recv.at[1], peer),
        remote(b2, b2_peer, small_send.at[2], small_recv.at[2], peer),
    ]
    to_next = [
        remote(v.at[frames + f, arrived], v.at[f, arrived], x_send.at[f], x_recv.at[f], following)
        for f in range(BACK)
    ]
    own_z = remote(
        v.at[pl.ds(BACK, frames), arrived],
        v.at[pl.ds(BACK, frames), halo_there],
        own_send, own_recv, z_peer,
    )
    forward_z = [
        remote(v.at[f, arrived], v.at[f, halo_there], z_send.at[f], z_recv.at[f], z_peer)
        for f in range(BACK)
    ]
    forward_p = [
        remote(v.at[f, arrived], v.at[f, inner_there], p_send.at[f], p_recv.at[f], peer)
        for f in range(BACK)
    ]

    small[0].start()

    @pl.when(has_next)
    def _():
        for f in reversed(range(BACK)):
            to_next[f].start()

    @pl.when(has_z)
    def _():
        own_z.start()

    small[1].start()
    small[2].start()
    for copy in w2_copies:
        copy.start()

    @pl.when(no_z)
    def _():
        v[:, halo_here] = jnp.zeros((v.shape[0], half, columns, channels), v.dtype)

    def pass_on(f):
        @pl.when(has_prev)
        def _():
            remote(v.at[f, arrived], v.at[f, arrived], x_send.at[f], x_recv.at[f], preceding).wait_recv()
            forward_p[f].start()

            @pl.when(has_z)
            def _():
                forward_z[f].start()

    def inner_ready(f):
        @pl.when(has_prev)
        def _():
            remote(v.at[f, arrived], v.at[f, inner_here], p_send.at[f], p_recv.at[f], peer).wait_recv()

    def outer_ready(f):
        @pl.when(jnp.logical_and(has_prev, has_z))
        def _():
            remote(v.at[f, arrived], v.at[f, halo_here], z_send.at[f], z_recv.at[f], z_peer).wait_recv()

    def taps(source, index, first, count, oldest=0):
        return jnp.concatenate(
            [
                source[index + a, pl.ds(first + b, count)].reshape(count * columns, channels)
                for a in range(oldest, 3)
                for b in range(3)
            ],
            axis=1,
        )

    def shifted_sum(parts, width, bias):
        size = parts.shape[0]
        column = lax.broadcasted_iota(jnp.int32, (size, width), 0) % columns
        before = pltpu.roll(parts[:, 0:width], 1, 0)
        after = pltpu.roll(parts[:, 2 * width : 3 * width], size - 1, 0)
        total = parts[:, width : 2 * width] + jnp.where(column == 0, 0.0, before)
        total = total + jnp.where(column == columns - 1, 0.0, after) + bias
        return total / (1.0 + jnp.exp(-total))

    def hidden_rows(index, first, count, oldest=0):
        parts = lax.dot_general(
            taps(v, index - 2, first, count, oldest),
            jnp.concatenate([k1[tap].reshape(3 * channels, channels) for tap in range(3 * oldest, 9)], axis=1),
            (((1,), (1,)), ((), ())),
            preferred_element_type=jnp.float32,
        )
        bias = jnp.concatenate([b1[...], b1_peer[...]], axis=1)
        value = shifted_sum(parts, channels, bias).astype(h.dtype)
        h[index, pl.ds(first, count)] = value.reshape(count, columns, channels)

    def inner(index):
        hidden_rows(index, half * other, half)

    def outer(index):
        hidden_rows(index, half * core, half)
        clear_outside(index)

    def whole(index, oldest=0):
        hidden_rows(index, 0, rows, oldest)
        clear_outside(index)

    def clear_outside(index):
        @pl.when(no_z)
        def _():
            h[index, pl.ds((rows - 1) * core, 1)] = jnp.zeros((1, columns, channels), h.dtype)

    to_peer = [
        remote(going.at[t], out.at[t, mine], o_send.at[t], o_recv.at[t], peer)
        for t in range(frames // 2)
    ]

    def latent(t, oldest=0):
        parts = jnp.dot(
            taps(h, 2 * t, 0, half, oldest),
            k2[3 * oldest :].reshape((9 - 3 * oldest) * channels, 6 * width),
            preferred_element_type=jnp.float32,
        )
        for start, bias in ((width, b2_peer[...]), (0, b2[...])):
            chosen = jnp.concatenate(
                [
                    parts[:, 2 * width * e + start : 2 * width * e + start + width]
                    for e in range(3)
                ],
                axis=1,
            )
            value = shifted_sum(chosen, width, bias).astype(out.dtype).reshape(half, columns, width)
            if start:
                going[t] = value
                to_peer[t].start()
            else:
                out[t, mine] = value

    small[0].wait_recv()
    small[1].wait_recv()
    small[2].wait_recv()
    early = pl.ds(2 - core, 1)
    early_there = pl.ds((rows - 1) * core, 1)
    early_here = pl.ds((rows - 1) * other, 1)
    late = pl.ds(half * core, half)
    hand_early = [
        remote(h.at[frames + f, early], h.at[f, early], e_send.at[f], e_recv.at[f], following)
        for f in range(2)
    ]
    hand_late = [
        remote(h.at[frames + f, late], h.at[f, late], h_send.at[f], h_recv.at[f], following)
        for f in range(2)
    ]
    share = [
        remote(h.at[f, early], h.at[f, early_there], q_send.at[f], q_recv.at[f], peer)
        for f in range(2)
    ]

    inner(frames)

    @pl.when(has_next)
    def _():
        hand_early[0].start()
        inner(frames + 1)
        hand_early[1].start()

    pass_on(1)

    @pl.when(has_z)
    def _():
        remote(
            v.at[pl.ds(BACK, frames), halo_here], v.at[pl.ds(BACK, frames), halo_here],
            own_send, own_recv, z_peer,
        ).wait_recv()

    outer(frames)

    @pl.when(has_next)
    def _():
        hand_late[0].start()
        outer(frames + 1)
        hand_late[1].start()

    pass_on(0)
    for index in range(frames - 1, 3, -1):
        whole(index)

    @pl.when(has_prev)
    def _():
        inner_ready(1)
        inner(3)
        outer_ready(1)
        outer(3)
        for f in range(2):
            remote(h.at[f, early], h.at[f, early], e_send.at[f], e_recv.at[f], preceding).wait_recv()
            share[f].start()
        inner_ready(0)
        inner(2)
        outer_ready(0)
        outer(2)

    @pl.when(slab == 0)
    def _():
        whole(3, 1)
        whole(2, 2)

    for copy in w2_copies:
        copy.wait()
    for t in range(1, frames // 2):
        latent(t)

    @pl.when(has_prev)
    def _():
        for f in range(2):
            remote(h.at[f, early], h.at[f, early_here], q_send.at[f], q_recv.at[f], peer).wait_recv()
            remote(h.at[f, late], h.at[f, late], h_send.at[f], h_recv.at[f], preceding).wait_recv()
            shared = h[f, early_here].reshape(columns, channels)
            shared = jnp.concatenate([shared[:, part:], shared[:, :part]], axis=1)
            h[f, early_here] = shared.reshape(1, columns, channels)
        latent(0)

    @pl.when(slab == 0)
    def _():
        latent(0, 2)

    for copy in small:
        copy.wait_send()

    @pl.when(has_next)
    def _():
        for copy in to_next:
            copy.wait_send()
        for copy in hand_early + hand_late:
            copy.wait_send()

    @pl.when(has_z)
    def _():
        own_z.wait_send()

    @pl.when(has_prev)
    def _():
        for copy in forward_p + share:
            copy.wait_send()

        @pl.when(has_z)
        def _():
            for copy in forward_z:
                copy.wait_send()

    theirs = pl.ds(half * other, half)
    for t in range(frames // 2):
        remote(going.at[t], out.at[t, theirs], o_send.at[t], o_recv.at[t], peer).wait_recv()
        to_peer[t].wait_send()


def shards(tiles, slabs, video, first_weight, first_bias, second_weight, second_bias):
    frames, rows, columns, channels = video.shape
    half = rows // 2
    assert half == 2 and frames >= 4 and frames % 2 == 0
    part = first_bias.shape[0]
    width = second_bias.shape[0]
    anywhere = pl.BlockSpec(memory_space=pltpu.HBM)
    inside = pl.BlockSpec(memory_space=pltpu.VMEM)
    dma = pltpu.SemaphoreType.DMA
    return pl.pallas_call(
        functools.partial(kernel, tiles, slabs),
        out_shape=jax.ShapeDtypeStruct((frames // 2, rows, columns, width), jnp.bfloat16),
        in_specs=[anywhere, anywhere, inside, anywhere, inside],
        out_specs=inside,
        scratch_shapes=[
            pltpu.VMEM((BACK + frames, rows + 2, columns, channels), jnp.bfloat16),
            pltpu.VMEM((frames + 2, half + 2, columns, channels), jnp.bfloat16),
            pltpu.VMEM((9, 3, 2, part, channels), jnp.bfloat16),
            pltpu.VMEM((9, channels, 6 * width), jnp.bfloat16),
            pltpu.VMEM((1, part), jnp.float32),
            pltpu.VMEM((1, width), jnp.float32),
            pltpu.VMEM((frames // 2, half, columns, width), jnp.bfloat16),
            dma, dma, dma((12,)), dma((2,)), dma((2,)), dma((2,)), dma((2,)), dma((2,)), dma((2,)), dma((3,)), dma((3,)), dma, dma,
            dma((BACK,)), dma((BACK,)), dma((BACK,)), dma((BACK,)), dma((BACK,)), dma((BACK,)),
            dma((frames // 2,)), dma((frames // 2,)),
        ],
        compiler_params=pltpu.CompilerParams(
            collective_id=0, has_side_effects=True, vmem_limit_bytes=32 << 20
        ),
    )(
        *(
            pltpu.with_memory_space_constraint(operand, pltpu.HBM)
            for operand in (
                video,
                jnp.swapaxes(first_weight, 3, 4).reshape(9, 3, part, channels),
                first_bias.reshape(1, part),
                second_weight.reshape(9, 3, channels, 2 * width),
                second_bias.reshape(1, width),
            )
        )
    )


def solution(mesh):
    placed = (
        P(("clip", "slab"), "tile", None, None),
        P(None, None, None, None, "chan"),
        P("chan"),
        P(),
        P("chan"),
    )
    return jax.shard_map(
        functools.partial(shards, mesh.shape["tile"], mesh.shape["slab"]),
        mesh=mesh,
        in_specs=placed,
        out_specs=P(("clip", "slab"), "tile", None, "chan"),
        check_vma=False,
    )
```

profile of v0, /device:TPU:19, one launch (start us, length us, event | category | flops | bytes accessed | tf_op | source)
XLA Modules:
  0.0 15.3 jit_solution(512401131084866791)
XLA Ops:
  0.0 14.6 %shard_map.55 = bf16[2,4,128,128]{3,2,1,0:T(8,128)(2,1)S(1)} custom-call(bf16[4,4,128,128]{3,2,1,0:T(8,128)(2,1)} %video.1, bf16[9,3,64,128]{3,2,1,0:T(8,128)(2,1)} %bitcast.7, f32[1,64]{1,0:T(1,128)} %bitcast.8, bf16[9,3,128,256]{3,2,1,0:T(8,128)(2,1)} %bitcast.6, f32[1,128]{1,0:T(1,128)} %bitcast.9), custom_call_target="tpu_custom_call" | custom-call | tf_op jit(solution)/shard_map/pallas_call | solution.py:351
  14.6 0.7 %copy.7 = bf16[2,4,128,128]{3,2,1,0:T(8,128)(2,1)} copy(bf16[2,4,128,128]{3,2,1,0:T(8,128)(2,1)S(1)} %shard_map.55) | data formatting | bytes 524288
where the time goes:
time: 15.5 us; the launch traced here: 15.3 us
  Pallas kernels  14.6 us (94%)
  local copies, waits for them, and re-layouts  0.71 us (5%)
    pallas_call x1, Pallas kernels, shards(): pl.pallas_call(functools.partial(kernel, tiles, slabs), out_shape=jax.Sha...  14.6 us
    unnamed x1, local copies, waits for them, and re-layouts  0.71 us

commit v1 on v0

v1 whole, which is shorter than its diff:
```python
import functools

import jax
import jax.numpy as jnp
from jax import lax
from jax.experimental import pallas as pl
from jax.experimental.pallas import tpu as pltpu
from jax.sharding import PartitionSpec as P

MESH = pl.DeviceIdType.MESH
BACK = 2


def kernel(
    tiles, slabs, video, w1, b1, w2, b2, out,
    v, h, k1, k2, bias1, bias2, pieces, incoming, going, going0, sum0, acc,
    load, w1_s, w1_r, b_s, b_r, x_s, x_r, z_s, z_r, p_s, p_r, f_s, f_r, q_s, q_r, o_s, o_r,
):
    frames, rows, columns, channels = video.shape
    half = rows // 2
    width = b2.shape[1]
    core = lax.axis_index("chan")
    tile = lax.axis_index("tile")
    slab = lax.axis_index("slab")
    other = 1 - core
    z_tile = tile + 2 * core - 1
    has_z = jnp.logical_and(z_tile >= 0, z_tile < tiles)
    no_z = jnp.logical_or(z_tile < 0, z_tile >= tiles)
    has_next = slab < slabs - 1
    no_next = slab == slabs - 1
    has_prev = slab > 0
    no_prev = slab == 0
    peer = {"chan": other}
    z_peer = {"chan": other, "tile": z_tile}
    next_same = {"slab": slab + 1}
    next_cross = {"slab": slab + 1, "chan": other}
    prev_same = {"slab": slab - 1}
    prev_cross = {"slab": slab - 1, "chan": other}

    def when(condition, body):
        if condition is None:
            body()
        else:
            pl.when(condition)(body)

    barrier = pltpu.get_barrier_semaphore()
    everyone = (
        (None, peer), (has_z, z_peer), (has_next, next_same), (has_next, next_cross),
        (has_prev, prev_same), (has_prev, prev_cross),
    )
    for condition, device in everyone:
        when(condition, lambda device=device: pl.semaphore_signal(
            barrier, inc=1, device_id=device, device_id_type=MESH))
    met = 1 + sum(jnp.where(condition, 1, 0) for condition, _ in everyone[1:])

    into_v = pltpu.make_async_copy(video, v.at[pl.ds(BACK, frames), pl.ds(half * other, rows)], load.at[0])
    own_w1 = pltpu.make_async_copy(w1, k1.at[:, :, core], load.at[1])
    own_b1 = pltpu.make_async_copy(b1, bias1.at[core], load.at[2])
    own_b2 = pltpu.make_async_copy(b2, bias2.at[0], load.at[3])
    own_w2 = [
        pltpu.make_async_copy(
            w2.at[:, :, :, pl.ds(pl.multiple_of(owner * width, width), width)], k2.at[n], load.at[4 + n])
        for n, owner in enumerate((core, other))
    ]
    for copy in (into_v, own_w1, own_b1, own_b2):
        copy.start()

    def remote(src, dst, send, recv, device):
        return pltpu.make_async_remote_copy(
            src_ref=src, dst_ref=dst, send_sem=send, recv_sem=recv,
            device_id=device, device_id_type=MESH,
        )

    mine = pl.ds(half * core, half)
    theirs = pl.ds(half * other, half)
    arrived = pl.ds(half, half)
    halo_here = pl.ds(rows * core, half)
    halo_there = pl.ds(rows * other, half)
    inner_here = pl.ds(rows * other, half)
    inner_there = pl.ds(rows * core, half)
    early_frames = pl.ds(BACK, frames - 1)
    late_frame = pl.ds(BACK + frames - 1, 1)
    near_here = pl.ds(1 + (rows - 1) * core, 1)
    near_there = pl.ds(1 + (rows - 1) * other, 1)
    far_here = pl.ds((rows + 1) * core, 1)
    far_there = pl.ds((rows + 1) * other, 1)
    near_row = pl.ds((rows - 1) * core, 1)
    far_row = pl.ds(half - 1 + core, 1)

    to_next = [
        remote(video.at[frames - BACK + f, theirs], v.at[f, arrived], x_s.at[f], x_r.at[f], next_cross)
        for f in range(BACK)
    ]

    def z_copies(near, far):
        return [
            remote(video.at[pl.ds(0, frames - 1), near[0]], v.at[early_frames, near[1]], z_s.at[0], z_r.at[0], z_peer),
            remote(video.at[pl.ds(frames - 1, 1), near[0]], v.at[late_frame, near[1]], z_s.at[1], z_r.at[1], z_peer),
            remote(video.at[pl.ds(0, frames - 1), far[0]], v.at[early_frames, far[1]], z_s.at[2], z_r.at[2], z_peer),
            remote(video.at[pl.ds(frames - 1, 1), far[0]], v.at[late_frame, far[1]], z_s.at[3], z_r.at[3], z_peer),
        ]

    z_out = z_copies((near_row, near_there), (far_row, far_there))
    z_in = z_copies((near_row, near_here), (far_row, far_here))
    forward_p = [
        remote(v.at[f, arrived], v.at[f, inner_there], p_s.at[f], p_r.at[f], peer) for f in range(BACK)
    ]
    forward_z = [
        remote(v.at[f, arrived], v.at[f, halo_there], f_s.at[f], f_r.at[f], z_peer) for f in range(BACK)
    ]
    to_peer = [
        remote(w1, k1.at[:, :, core], w1_s, w1_r, peer),
        remote(b1, bias1.at[core], b_s.at[0], b_r.at[0], peer),
        remote(b2, bias2.at[1], b_s.at[1], b_r.at[1], peer),
    ]

    with jax.named_scope("entrybar"):
        pl.semaphore_wait(barrier, met)

    @pl.when(has_next)
    def _():
        to_next[1].start()

    @pl.when(has_z)
    def _():
        z_out[0].start()

    @pl.when(jnp.logical_and(has_z, has_next))
    def _():
        z_out[1].start()

    to_peer[0].start()

    @pl.when(has_next)
    def _():
        to_next[0].start()

    @pl.when(has_z)
    def _():
        z_out[2].start()

    @pl.when(jnp.logical_and(has_z, has_next))
    def _():
        z_out[3].start()

    to_peer[1].start()
    to_peer[2].start()
    for copy in own_w2:
        copy.start()

    @pl.when(no_z)
    def _():
        v[:, halo_here] = jnp.zeros((v.shape[0], half, columns, channels), v.dtype)

    def taps(source, index, first, count, steps):
        return jnp.concatenate(
            [
                source[index + a, pl.ds(first + b, count)].reshape(count * columns, channels)
                for a in steps
                for b in range(3)
            ],
            axis=1,
        )

    def shifted(parts, size):
        column = lax.broadcasted_iota(jnp.int32, (parts.shape[0], size), 0) % columns
        before = pltpu.roll(parts[:, 0:size], 1, 0)
        after = pltpu.roll(parts[:, 2 * size : 3 * size], parts.shape[0] - 1, 0)
        total = parts[:, size : 2 * size] + jnp.where(column == 0, 0.0, before)
        return total + jnp.where(column == columns - 1, 0.0, after)

    def silu(total):
        return total / (1.0 + jnp.exp(-total))

    def hidden(indices, first, count, oldest=0):
        parts = lax.dot_general(
            jnp.concatenate([taps(v, index - 2, first, count, range(oldest, 3)) for index in indices], axis=0),
            jnp.concatenate([k1[tap].reshape(3 * channels, channels) for tap in range(3 * oldest, 9)], axis=1),
            (((1,), (1,)), ((), ())),
            preferred_element_type=jnp.float32,
        )
        bias = jnp.concatenate([bias1[0], bias1[1]], axis=1)
        value = silu(shifted(parts, channels) + bias).astype(h.dtype)
        value = value.reshape(len(indices), count, columns, channels)
        for n, index in enumerate(indices):
            h[index, pl.ds(first, count)] = value[n]

    def inner(*indices, oldest=0):
        with jax.named_scope("inner" + "_".join(map(str, indices))):
            hidden(indices, half * other, half, oldest)

    def clear_outside(index):
        @pl.when(no_z)
        def _():
            h[index, pl.ds((rows - 1) * core, 1)] = jnp.zeros((1, columns, channels), h.dtype)

    def outer(*indices, oldest=0):
        with jax.named_scope("outer" + "_".join(map(str, indices))):
            hidden(indices, half * core, half, oldest)
            for index in indices:
                clear_outside(index)

    def near(*indices):
        with jax.named_scope("near"):
            hidden(indices, 1 + core, 1)

    def far(*indices):
        with jax.named_scope("far"):

            @pl.when(has_z)
            def _():
                hidden(indices, (rows - 1) * core, 1)

            for index in indices:
                clear_outside(index)

    def second(index, first, count, steps):
        matrix = jnp.concatenate(
            [
                jnp.concatenate([k2[n, 3 * a + b, e] for e in range(3) for n in range(2)], axis=1)
                for a in steps
                for b in range(3)
            ],
            axis=0,
        )
        parts = jnp.dot(taps(h, index, first, count, steps), matrix, preferred_element_type=jnp.float32)
        return [
            shifted(
                jnp.concatenate(
                    [parts[:, (2 * e + n) * width : (2 * e + n + 1) * width] for e in range(3)], axis=1
                ),
                width,
            )
            for n in range(2)
        ]

    def share(slot, local):
        place = half * core + local
        return [
            remote(pieces.at[slot, 0], incoming.at[place], q_s.at[2 * slot], q_r.at[place], next_same),
            remote(pieces.at[slot, 1], incoming.at[place], q_s.at[2 * slot + 1], q_r.at[place], next_cross),
        ]

    shares = [share(0, other), share(1, core)]

    def send_share(slot, local):
        with jax.named_scope("share%d" % slot):
            both = second(frames, local, 1, range(0, 2))
            for n in (1, 0):
                pieces[slot, n] = both[n].astype(pieces.dtype)
                shares[slot][n].start()

    result = [
        remote(going.at[t - 1], out.at[t, mine], o_s.at[t], o_r.at[t], peer) for t in range(1, frames // 2)
    ]
    part0 = remote(going0, sum0.at[mine], o_s.at[0], o_r.at[0], peer)

    def finish(t, both):
        going[t - 1] = silu(both[1] + bias2[1]).astype(out.dtype).reshape(half, columns, width)
        result[t - 1].start()
        out[t, mine] = silu(both[0] + bias2[0]).astype(out.dtype).reshape(half, columns, width)

    def latent(t):
        with jax.named_scope("latent%d" % t):
            finish(t, second(2 * t, 0, half, range(3)))

    def first_latent():
        with jax.named_scope("latent0"):
            both = second(0, 0, half, range(2, 3))
            going0[...] = both[1].reshape(half, columns, width)
            part0.start()
            sum0[mine] = both[0].reshape(half, columns, width)

    def wait_z(which):
        with jax.named_scope("zwait%d" % which):

            @pl.when(has_z)
            def _():
                z_in[which].wait_recv()

    def pass_on(f):
        with jax.named_scope("pass%d" % f):

            @pl.when(has_prev)
            def _():
                remote(
                    video.at[frames - BACK + f, theirs], v.at[f, arrived], x_s.at[f], x_r.at[f], prev_cross
                ).wait_recv()
                forward_p[f].start()

                @pl.when(has_z)
                def _():
                    forward_z[f].start()

    def inner_ready(f):
        with jax.named_scope("pwait%d" % f):
            remote(v.at[f, arrived], v.at[f, inner_here], p_s.at[f], p_r.at[f], peer).wait_recv()

    def outer_ready(f):
        with jax.named_scope("fwait%d" % f):

            @pl.when(has_z)
            def _():
                remote(v.at[f, arrived], v.at[f, halo_here], f_s.at[f], f_r.at[f], z_peer).wait_recv()

    with jax.named_scope("loadwait"):
        into_v.wait()
        own_w1.wait()
        own_b1.wait()
        own_b2.wait()
    with jax.named_scope("w1wait"):
        remote(w1, k1.at[:, :, other], w1_s, w1_r, peer).wait_recv()
        remote(b1, bias1.at[other], b_s.at[0], b_r.at[0], peer).wait_recv()
        to_peer[2].wait_recv()

    last = frames + 1

    @pl.when(has_next)
    def _():
        inner(frames, last)

    @pl.when(no_next)
    def _():
        inner(frames)

    @pl.when(no_prev)
    def _():
        inner(3, oldest=1)
        inner(2, oldest=2)

    pass_on(1)
    wait_z(0)

    @pl.when(has_next)
    def _():
        wait_z(1)
        near(frames, last)
        with jax.named_scope("w2wait"):
            for copy in own_w2:
                copy.wait()
        send_share(0, other)

    wait_z(2)

    @pl.when(no_next)
    def _():
        outer(frames)
        with jax.named_scope("w2wait"):
            for copy in own_w2:
                copy.wait()

    pass_on(0)

    @pl.when(has_next)
    def _():
        wait_z(3)
        far(frames, last)
        send_share(1, core)

    for index in range(frames - 1, 3, -1):
        inner(index)
        outer(index)
    for t in range(2, frames // 2):
        latent(t)

    @pl.when(no_prev)
    def _():
        outer(3, oldest=1)
        outer(2, oldest=2)
        first_latent()
        latent(1)

    @pl.when(has_prev)
    def _():
        inner_ready(1)
        inner(3)
        inner_ready(0)
        inner(2)
        outer_ready(1)
        outer(3)
        with jax.named_scope("latent1a"):
            both = second(2, 0, half, range(1, 3))
            for n in range(2):
                acc[n] = both[n]
        outer_ready(0)
        outer(2)
        first_latent()
        with jax.named_scope("latent1b"):
            both = second(2, 0, half, range(0, 1))
            finish(1, [acc[n] + both[n] for n in range(2)])

    with jax.named_scope("part0"):
        remote(going0, sum0.at[theirs], o_s.at[0], o_r.at[0], peer).wait_recv()

    def close(first, count, extra):
        total = sum0[pl.ds(first, count)].reshape(count * columns, width)
        if extra:
            total = total + incoming[pl.ds(first, count)].reshape(count * columns, width).astype(jnp.float32)
        out[0, pl.ds(first, count)] = silu(total + bias2[0]).astype(out.dtype).reshape(count, columns, width)

    @pl.when(has_prev)
    def _():
        for row in (1, 2, 0, 3):
            with jax.named_scope("close%d" % row):
                remote(pieces.at[0, 0], incoming.at[row], q_s.at[0], q_r.at[row], prev_same).wait_recv()
                close(row, 1, True)

    @pl.when(no_prev)
    def _():
        close(0, rows, False)

    with jax.named_scope("ends"):
        for copy in to_peer:
            copy.wait_send()
        part0.wait_send()
        for t in range(1, frames // 2):
            remote(going.at[t - 1], out.at[t, theirs], o_s.at[t], o_r.at[t], peer).wait_recv()
            result[t - 1].wait_send()

        @pl.when(has_next)
        def _():
            for copy in to_next + shares[0] + shares[1]:
                copy.wait_send()

        @pl.when(has_z)
        def _():
            z_out[0].wait_send()
            z_out[2].wait_send()

        @pl.when(jnp.logical_and(has_z, has_next))
        def _():
            z_out[1].wait_send()
            z_out[3].wait_send()

        @pl.when(has_prev)
        def _():
            for copy in forward_p:
                copy.wait_send()

        @pl.when(jnp.logical_and(has_prev, has_z))
        def _():
            for copy in forward_z:
                copy.wait_send()


def shards(tiles, slabs, video, first_weight, first_bias, second_weight, second_bias):
    frames, rows, columns, channels = video.shape
    half = rows // 2
    assert half == 2 and frames >= 4 and frames % 2 == 0
    part = first_bias.shape[0]
    width = second_bias.shape[0]
    anywhere = pl.BlockSpec(memory_space=pltpu.HBM)
    inside = pl.BlockSpec(memory_space=pltpu.VMEM)
    dma = pltpu.SemaphoreType.DMA
    vmem = pltpu.VMEM
    latents = frames // 2
    return pl.pallas_call(
        functools.partial(kernel, tiles, slabs),
        out_shape=jax.ShapeDtypeStruct((latents, rows, columns, width), jnp.bfloat16),
        in_specs=[anywhere] * 5,
        out_specs=inside,
        scratch_shapes=[
            vmem((BACK + frames, rows + 2, columns, channels), jnp.bfloat16),
            vmem((frames + 2, half + 2, columns, channels), jnp.bfloat16),
            vmem((9, 3, 2, part, channels), jnp.bfloat16),
            vmem((2, 9, 3, channels, width), jnp.bfloat16),
            vmem((2, 1, part), jnp.float32),
            vmem((2, 1, width), jnp.float32),
            vmem((2, 2, columns, width), jnp.bfloat16),
            vmem((rows, columns, width), jnp.bfloat16),
            vmem((latents - 1, half, columns, width), jnp.bfloat16),
            vmem((half, columns, width), jnp.float32),
            vmem((rows, columns, width), jnp.float32),
            vmem((2, half * columns, width), jnp.float32),
            dma((6,)), dma, dma, dma((2,)), dma((2,)), dma((BACK,)), dma((BACK,)), dma((4,)), dma((4,)),
            dma((BACK,)), dma((BACK,)), dma((BACK,)), dma((BACK,)), dma((4,)), dma((rows,)),
            dma((latents,)), dma((latents,)),
        ],
        compiler_params=pltpu.CompilerParams(
            collective_id=0, has_side_effects=True, vmem_limit_bytes=32 << 20
        ),
    )(
        *(
            pltpu.with_memory_space_constraint(operand, pltpu.HBM)
            for operand in (
                video,
                jnp.swapaxes(first_weight, 3, 4).reshape(9, 3, part, channels),
                first_bias.reshape(1, part),
                second_weight.reshape(9, 3, channels, 2 * width),
                second_bias.reshape(1, width),
            )
        )
    )


def solution(mesh):
    placed = (
        P(("clip", "slab"), "tile", None, None),
        P(None, None, None, None, "chan"),
        P("chan"),
        P(),
        P("chan"),
    )
    return jax.shard_map(
        functools.partial(shards, mesh.shape["tile"], mesh.shape["slab"]),
        mesh=mesh,
        in_specs=placed,
        out_specs=P(("clip", "slab"), "tile", None, "chan"),
        check_vma=False,
    )
```

time: 15.5 us -> 14 us (0.903)
  the two profiles are of different devices: /device:TPU:19 before, /device:TPU:0 now
where the time goes in v1:
time: 14 us; the launch traced here: 13.8 us
  Pallas kernels  13.1 us (94%)
  local copies, waits for them, and re-layouts  0.71 us (5%)
    pallas_call x1, Pallas kernels, shards(): pl.pallas_call(functools.partial(kernel, tiles, slabs), out_shape=jax.Sha...  13.1 us
    unnamed x1, local copies, waits for them, and re-layouts  0.71 us

profile of v1, /device:TPU:0, one launch (start us, length us, event | category | flops | bytes accessed | tf_op | source)
XLA Modules:
  0.0 13.8 jit_solution(5502615968251969619)
XLA Ops:
  0.0 13.1 %shard_map.55 = bf16[2,4,128,128]{3,2,1,0:T(8,128)(2,1)S(1)} custom-call(bf16[4,4,128,128]{3,2,1,0:T(8,128)(2,1)} %video.1, bf16[9,3,64,128]{3,2,1,0:T(8,128)(2,1)} %bitcast.7, f32[1,64]{1,0:T(1,128)} %bitcast.8, bf16[9,3,128,256]{3,2,1,0:T(8,128)(2,1)} %bitcast.6, f32[1,128]{1,0:T(1,128)} %bitcast.9), custom_call_target="tpu_custom_call" | custom-call | tf_op jit(solution)/shard_map/pallas_call | solution.py:457
  13.1 0.7 %copy.7 = bf16[2,4,128,128]{3,2,1,0:T(8,128)(2,1)} copy(bf16[2,4,128,128]{3,2,1,0:T(8,128)(2,1)S(1)} %shard_map.55) | data formatting | bytes 524288

commit v2 on v1

v2 whole, which is shorter than its diff:
```python
import functools

import jax
import jax.numpy as jnp
from jax import lax
from jax.experimental import pallas as pl
from jax.experimental.pallas import tpu as pltpu
from jax.sharding import PartitionSpec as P

MESH = pl.DeviceIdType.MESH
BACK = 2


def kernel(
    tiles, slabs, video, w1, b1, w2, b2, out,
    v, h, k1, k2, bias1, bias2, pieces, incoming, going, going0, sum0, acc,
    load, w_s, b_s, x_s, z_s, p_s, q_s, o_s, w1_r, b_r, x_r, z_r, p_r, h_r, f_r, q_r, o_r,
):
    frames, rows, columns, channels = video.shape
    half = rows // 2
    width = b2.shape[1]
    core = lax.axis_index("chan")
    tile = lax.axis_index("tile")
    slab = lax.axis_index("slab")
    other = 1 - core
    z_tile = tile + 2 * core - 1
    has_z = jnp.logical_and(z_tile >= 0, z_tile < tiles)
    no_z = jnp.logical_or(z_tile < 0, z_tile >= tiles)
    has_next = slab < slabs - 1
    no_next = slab == slabs - 1
    has_prev = slab > 0
    no_prev = slab == 0
    one = core == 1
    zero = core == 0
    above = tile > 0
    below = tile < tiles - 1
    peer = {"chan": other}
    z_minus = {"tile": tile - 1, "chan": 1}
    z_plus = {"tile": tile + 1, "chan": 0}
    next_same = {"slab": slab + 1}
    next_cross = {"slab": slab + 1, "chan": other}
    prev_same = {"slab": slab - 1}

    def both(*conditions):
        return functools.reduce(jnp.logical_and, conditions)

    def when(condition, body):
        if condition is None:
            body()
        else:
            pl.when(condition)(body)

    barrier = pltpu.get_barrier_semaphore()
    greetings = (
        (None, peer),
        (has_z, {"chan": other, "tile": z_tile}),
        (has_prev, {"slab": slab - 1, "chan": 1}),
    )
    for condition, device in greetings:
        when(condition, lambda device=device: pl.semaphore_signal(
            barrier, inc=1, device_id=device, device_id_type=MESH))
    met = 1
    for condition, count in ((has_z, 1), (both(one, has_next), 2)):
        met = met + jnp.where(condition, count, 0)

    into_v = pltpu.make_async_copy(video, v.at[pl.ds(BACK, frames), pl.ds(half * other, rows)], load.at[0])
    own_w1 = pltpu.make_async_copy(w1, k1.at[:, :, core], load.at[1])
    own_b1 = pltpu.make_async_copy(b1, bias1.at[core], load.at[2])
    own_b2 = pltpu.make_async_copy(b2, bias2.at[0], load.at[4])
    own_w2 = [
        pltpu.make_async_copy(
            w2.at[:, :, :, pl.ds(pl.multiple_of(owner * width, width), width)], k2.at[n], load.at[3])
        for n, owner in enumerate((core, other))
    ]
    for copy in (into_v, own_w1, own_b1, own_b2):
        copy.start()

    def remote(src, dst, send, recv, device):
        return pltpu.make_async_remote_copy(
            src_ref=src, dst_ref=dst, send_sem=send, recv_sem=recv,
            device_id=device, device_id_type=MESH,
        )

    def wait_bytes(ref, semaphore):
        pltpu.make_async_copy(ref, ref, semaphore).wait()

    mine = pl.ds(half * core, half)
    theirs = pl.ds(half * other, half)
    halo_here = pl.ds(rows * core, half)
    frame0, frame1 = frames, frames + 1

    low, high = pl.ds(0, half), pl.ds(half, half)
    halo_low, halo_high = pl.ds(0, half), pl.ds(rows, half)

    def x_copies(device):
        return [
            [
                remote(v.at[frames + f, some], v.at[f, some], x_s, x_r.at[2 * f + n], device)
                for n, some in enumerate((low, high))
            ]
            for f in range(BACK)
        ]

    x_out = x_copies(next_same)
    x_in = x_copies(prev_same)
    forward_z = [
        [
            (above, remote(v.at[f, low], v.at[f, halo_high], z_s.at[0], f_r.at[f], z_minus)),
            (below, remote(v.at[f, high], v.at[f, halo_low], z_s.at[1], f_r.at[f], z_plus)),
        ]
        for f in range(BACK)
    ]
    f_in = [remote(v.at[f, low], v.at[f, halo_low], z_s.at[0], f_r.at[f], peer) for f in range(BACK)]
    forward_p = [remote(v.at[f, low], v.at[f, pl.ds(half, half)], p_s, p_r.at[f], peer) for f in range(BACK)]
    forward_h = [
        remote(h.at[BACK + f, low], h.at[BACK + f, pl.ds(half, half)], p_s, h_r.at[f], peer) for f in range(BACK)
    ]

    def z_copies(count):
        some = pl.ds(BACK, count)
        return [
            [
                remote(video.at[pl.ds(0, count), pl.ds(n, 1)], v.at[some, pl.ds(rows + n, 1)], z_s.at[0], z_r.at[n], z_minus)
                for n in range(half)
            ],
            [
                remote(
                    v.at[some, pl.ds(rows - 1 - n, 1)], v.at[some, pl.ds(half - 1 - n, 1)], z_s.at[1], z_r.at[n], z_plus
                )
                for n in range(half)
            ],
        ]

    z_full = z_copies(frames)
    z_short = z_copies(frames - 1)

    def start_z(side):
        for condition, copies in ((has_next, z_full), (no_next, z_short)):

            @pl.when(condition)
            def _():
                for copy in copies[side]:
                    copy.start()

    to_peer = [
        remote(w1, k1.at[:, :, core], w_s, w1_r, peer),
        remote(b1, bias1.at[core], b_s.at[0], b_r.at[0], peer),
        remote(b2, bias2.at[1], b_s.at[1], b_r.at[1], peer),
    ]

    with jax.named_scope("entrybar"):
        pl.semaphore_wait(barrier, met)

    @pl.when(both(zero, above))
    def _():
        start_z(0)

    for copy in to_peer:
        copy.start()
    with jax.named_scope("loadwait"):
        into_v.wait()

    @pl.when(one)
    def _():
        @pl.when(has_next)
        def _():
            for n in range(2):
                for f in (1, 0):
                    x_out[f][n].start()

        @pl.when(below)
        def _():
            start_z(1)

    for copy in own_w2:
        copy.start()

    @pl.when(no_z)
    def _():
        v[:, halo_here] = jnp.zeros((v.shape[0], half, columns, channels), v.dtype)

    def taps(source, index, first, count, steps):
        return jnp.concatenate(
            [
                source[index + a, pl.ds(first + b, count)].reshape(count * columns, channels)
                for a in steps
                for b in range(3)
            ],
            axis=1,
        )

    def shifted(parts, size):
        column = lax.broadcasted_iota(jnp.int32, (parts.shape[0], size), 0) % columns
        before = pltpu.roll(parts[:, 0:size], 1, 0)
        after = pltpu.roll(parts[:, 2 * size : 3 * size], parts.shape[0] - 1, 0)
        total = parts[:, size : 2 * size] + jnp.where(column == 0, 0.0, before)
        return total + jnp.where(column == columns - 1, 0.0, after)

    def silu(total):
        return total / (1.0 + jnp.exp(-total))

    def hidden(indices, first, count, oldest=0):
        parts = lax.dot_general(
            jnp.concatenate([taps(v, index - 2, first, count, range(oldest, 3)) for index in indices], axis=0),
            jnp.concatenate([k1[tap].reshape(3 * channels, channels) for tap in range(3 * oldest, 9)], axis=1),
            (((1,), (1,)), ((), ())),
            preferred_element_type=jnp.float32,
        )
        bias = jnp.concatenate([bias1[0], bias1[1]], axis=1)
        value = silu(shifted(parts, channels) + bias).astype(h.dtype)
        value = value.reshape(len(indices), count, columns, channels)
        for n, index in enumerate(indices):
            h[index, pl.ds(first, count)] = value[n]

    def inner(*indices, oldest=0):
        with jax.named_scope("inner" + "_".join(map(str, indices))):
            hidden(indices, half * other, half, oldest)

    def clear_outside(index):
        @pl.when(no_z)
        def _():
            h[index, pl.ds((rows - 1) * core, 1)] = jnp.zeros((1, columns, channels), h.dtype)

    def outer(*indices, oldest=0):
        with jax.named_scope("outer" + "_".join(map(str, indices))):
            hidden(indices, half * core, half, oldest)
            for index in indices:
                clear_outside(index)

    def near(*indices):
        with jax.named_scope("near"):
            hidden(indices, 1 + core, 1)

    def far(*indices):
        with jax.named_scope("far"):

            @pl.when(has_z)
            def _():
                hidden(indices, (rows - 1) * core, 1)

            for index in indices:
                clear_outside(index)

    def second(index, first, count, steps, blocks):
        matrix = jnp.concatenate(
            [
                jnp.concatenate([k2[n, 3 * (a + shift) + b, e] for n, shift in blocks for e in range(3)], axis=1)
                for a in steps
                for b in range(3)
            ],
            axis=0,
        )
        parts = jnp.dot(taps(h, index, first, count, steps), matrix, preferred_element_type=jnp.float32)
        return [shifted(parts[:, 3 * k * width : 3 * (k + 1) * width], width) for k in range(len(blocks))]

    whole = ((0, 0), (1, 0))

    def share(slot, local):
        place = half * core + local
        return [
            remote(pieces.at[slot, 0], incoming.at[place], q_s, q_r.at[slot], next_same),
            remote(pieces.at[slot, 1], incoming.at[place], q_s, q_r.at[slot], next_cross),
        ]

    shares = [share(0, other), share(1, core)]

    def send_share(slot, local):
        with jax.named_scope("share%d" % slot):
            halves = second(frames, local, 1, range(0, 2), whole)
            for n in (1, 0):
                pieces[slot, n] = halves[n].astype(pieces.dtype)
                shares[slot][n].start()

    result = [
        remote(going.at[t - 1], out.at[t, mine], o_s, o_r.at[t], peer) for t in range(1, frames // 2)
    ]
    part0 = remote(going0, sum0.at[mine], o_s, o_r.at[0], peer)

    def latent(t):
        with jax.named_scope("latent%d" % t):
            own, away = second(2 * t, 0, half, range(3), whole)
            going[t - 1] = silu(away + bias2[1]).astype(out.dtype).reshape(half, columns, width)
            result[t - 1].start()
            out[t, mine] = silu(own + bias2[0]).astype(out.dtype).reshape(half, columns, width)

    def later_steps():
        with jax.named_scope("latent1a"):
            halves = second(2, 0, half, range(1, 3), whole)
            for n in range(2):
                acc[n] = halves[n]

    def last_steps():
        with jax.named_scope("tailA"):
            first, then = second(2, 0, half, range(0, 1), ((1, 2), (1, 0)))
            going0[...] = first.reshape(half, columns, width)
            part0.start()
            going[0] = silu(then + acc[1] + bias2[1]).astype(out.dtype).reshape(half, columns, width)
            result[0].start()
        with jax.named_scope("tailB"):
            first, then = second(2, 0, half, range(0, 1), ((0, 2), (0, 0)))
            sum0[mine] = first.reshape(half, columns, width)
            out[1, mine] = silu(then + acc[0] + bias2[0]).astype(out.dtype).reshape(half, columns, width)

    def wait_z(which, copies):
        with jax.named_scope("zwait%d" % which):

            @pl.when(has_z)
            def _():
                copies[0][which].wait_recv()

    def pass_on(f, n):
        with jax.named_scope("pass%d%d" % (f, n)):
            x_in[f][n].wait_recv()
            condition, copy = forward_z[f][n]
            pl.when(condition)(copy.start)
            if n == 0:
                forward_p[f].start()

    def from_peer(name, copy):
        @pl.when(zero)
        def _():
            with jax.named_scope(name):
                copy.wait_recv()

    def halo_ready(name, copy):
        with jax.named_scope(name):

            @pl.when(has_z)
            def _():
                copy.wait_recv()

    def w2_ready():
        with jax.named_scope("w2wait"):
            wait_bytes(k2, load.at[3])

    with jax.named_scope("loadwait"):
        own_w1.wait()
        own_b1.wait()
        own_b2.wait()
    with jax.named_scope("w1wait"):
        remote(w1, k1.at[:, :, other], w_s, w1_r, peer).wait_recv()
        remote(b1, bias1.at[other], b_s.at[0], b_r.at[0], peer).wait_recv()
        to_peer[2].wait_recv()

    last = frames + 1

    @pl.when(has_next)
    def _():
        inner(frames, last)

    @pl.when(no_next)
    def _():
        inner(frames)

    @pl.when(no_prev)
    def _():
        inner(3, oldest=1)
        inner(2, oldest=2)

    @pl.when(has_next)
    def _():
        wait_z(0, z_full)
        near(frames, last)
        w2_ready()

        send_share(0, other)
        wait_z(1, z_full)
        far(frames, last)
        send_share(1, core)

    def middle():
        for index in range(frames - 1, 3, -1):
            inner(index)
            outer(index)
        for t in range(2, frames // 2):
            latent(t)

    def own_last():
        @pl.when(no_next)
        def _():
            wait_z(0, z_short)
            wait_z(1, z_short)
            outer(frames)
            w2_ready()

    @pl.when(no_prev)
    def _():
        own_last()
        middle()
        outer(3, oldest=1)
        later_steps()
        outer(2, oldest=2)

    @pl.when(has_prev)
    def _():
        @pl.when(one)
        def _():
            pass_on(1, 0)
            pass_on(0, 0)
            pass_on(1, 1)
            inner(3)
            forward_h[1].start()
            pass_on(0, 1)
            inner(2)
            forward_h[0].start()

        own_last()
        middle()
        from_peer("pwait1", forward_p[1])
        halo_ready("fwait1", f_in[1])
        outer(3)
        from_peer("hwait1", forward_h[1])
        later_steps()
        from_peer("pwait0", forward_p[0])
        halo_ready("fwait0", f_in[0])
        outer(2)
        from_peer("hwait0", forward_h[0])

    last_steps()

    with jax.named_scope("part0"):
        remote(going0, sum0.at[theirs], o_s, o_r.at[0], peer).wait_recv()

    def close(first, count, extra):
        total = sum0[pl.ds(first, count)].reshape(count * columns, width)
        if extra:
            total = total + incoming[pl.ds(first, count)].reshape(count * columns, width).astype(jnp.float32)
        out[0, pl.ds(first, count)] = silu(total + bias2[0]).astype(out.dtype).reshape(count, columns, width)

    @pl.when(has_prev)
    def _():
        for slot, pair in enumerate(((half - 1, half), (0, rows - 1))):
            with jax.named_scope("close%d" % slot):
                wait_bytes(pieces.at[0], q_r.at[slot])
                for row in pair:
                    close(row, 1, True)

    @pl.when(no_prev)
    def _():
        close(0, rows, False)

    with jax.named_scope("ends"):
        for copy in to_peer:
            copy.wait_send()
        for t in range(1, frames // 2):
            remote(going.at[t - 1], out.at[t, theirs], o_s, o_r.at[t], peer).wait_recv()
        wait_bytes(v.at[pl.ds(0, frames // 2 + 1), low], o_s)

        @pl.when(has_next)
        def _():
            wait_bytes(incoming, q_s)

        @pl.when(both(one, has_next))
        def _():
            wait_bytes(v.at[pl.ds(0, BACK), pl.ds(0, rows)], x_s)

        @pl.when(both(one, has_prev))
        def _():
            wait_bytes(v.at[pl.ds(0, 2 * BACK), low], p_s)

        for side, condition in ((0, above), (1, below)):
            forwards = both(one, condition)
            for after, count in ((has_next, frames), (no_next, frames - 1)):
                if side == 0:

                    @pl.when(both(zero, condition, after))
                    def _():
                        wait_bytes(v.at[pl.ds(0, count), low], z_s.at[0])

                else:

                    @pl.when(both(forwards, after, no_prev))
                    def _():
                        wait_bytes(v.at[pl.ds(0, count), low], z_s.at[1])

                    @pl.when(both(forwards, after, has_prev))
                    def _():
                        wait_bytes(v.at[pl.ds(0, count + BACK), low], z_s.at[1])

            if side == 0:

                @pl.when(both(forwards, has_prev))
                def _():
                    wait_bytes(v.at[pl.ds(0, BACK), low], z_s.at[0])


def shards(tiles, slabs, video, first_weight, first_bias, second_weight, second_bias):
    frames, rows, columns, channels = video.shape
    half = rows // 2
    assert half == 2 and first_weight.shape[3] == channels == second_bias.shape[0] and frames >= 4 and frames % 2 == 0
    part = first_bias.shape[0]
    width = second_bias.shape[0]
    anywhere = pl.BlockSpec(memory_space=pltpu.HBM)
    inside = pl.BlockSpec(memory_space=pltpu.VMEM)
    dma = pltpu.SemaphoreType.DMA
    vmem = pltpu.VMEM
    latents = frames // 2
    return pl.pallas_call(
        functools.partial(kernel, tiles, slabs),
        out_shape=jax.ShapeDtypeStruct((latents, rows, columns, width), jnp.bfloat16),
        in_specs=[anywhere] * 5,
        out_specs=inside,
        scratch_shapes=[
            vmem((BACK + frames, rows + 2, columns, channels), jnp.bfloat16),
            vmem((frames + 2, half + 2, columns, channels), jnp.bfloat16),
            vmem((9, 3, 2, part, channels), jnp.bfloat16),
            vmem((2, 9, 3, channels, width), jnp.bfloat16),
            vmem((2, 1, part), jnp.float32),
            vmem((2, 1, width), jnp.float32),
            vmem((2, 2, columns, width), jnp.bfloat16),
            vmem((rows, columns, width), jnp.bfloat16),
            vmem((latents - 1, half, columns, width), jnp.bfloat16),
            vmem((half, columns, width), jnp.float32),
            vmem((rows, columns, width), jnp.float32),
            vmem((2, half * columns, width), jnp.float32),
            dma((5,)), dma, dma((2,)), dma, dma((2,)), dma, dma, dma, dma, dma((2,)), dma((2 * BACK,)), dma((2,)),
            dma((BACK,)), dma((BACK,)), dma((BACK,)), dma((2,)), dma((latents,)),
        ],
        compiler_params=pltpu.CompilerParams(
            collective_id=0, has_side_effects=True, vmem_limit_bytes=32 << 20
        ),
    )(
        *(
            pltpu.with_memory_space_constraint(operand, pltpu.HBM)
            for operand in (
                video,
                jnp.swapaxes(first_weight, 3, 4).reshape(9, 3, part, channels),
                first_bias.reshape(1, part),
                second_weight.reshape(9, 3, channels, 2 * width),
                second_bias.reshape(1, width),
            )
        )
    )


def solution(mesh):
    placed = (
        P(("clip", "slab"), "tile", None, None),
        P(None, None, None, None, "chan"),
        P("chan"),
        P(),
        P("chan"),
    )
    return jax.shard_map(
        functools.partial(shards, mesh.shape["tile"], mesh.shape["slab"]),
        mesh=mesh,
        in_specs=placed,
        out_specs=P(("clip", "slab"), "tile", None, "chan"),
        check_vma=False,
    )
```

time: 14 us -> 12 us (0.86)
  the two profiles are of different devices: /device:TPU:0 before, /device:TPU:19 now
where the time goes in v2:
time: 12 us; the launch traced here: 11.9 us
  Pallas kernels  11.2 us (93%)
  local copies, waits for them, and re-layouts  0.71 us (6%)
    pallas_call x1, Pallas kernels, shards(): pl.pallas_call(functools.partial(kernel, tiles, slabs), out_shape=jax.Sha...  11.2 us
    unnamed x1, local copies, waits for them, and re-layouts  0.71 us

profile of v2, /device:TPU:19, one launch (start us, length us, event | category | flops | bytes accessed | tf_op | source)
XLA Modules:
  0.0 11.9 jit_solution(9437643904770171701)
XLA Ops:
  0.0 11.2 %shard_map.55 = bf16[2,4,128,128]{3,2,1,0:T(8,128)(2,1)S(1)} custom-call(bf16[4,4,128,128]{3,2,1,0:T(8,128)(2,1)} %video.1, bf16[9,3,64,128]{3,2,1,0:T(8,128)(2,1)} %bitcast.7, f32[1,64]{1,0:T(1,128)} %bitcast.8, bf16[9,3,128,256]{3,2,1,0:T(8,128)(2,1)} %bitcast.6, f32[1,128]{1,0:T(1,128)} %bitcast.9), custom_call_target="tpu_custom_call" | custom-call | tf_op jit(solution)/shard_map/pallas_call | solution.py:498
  11.2 0.7 %copy.7 = bf16[2,4,128,128]{3,2,1,0:T(8,128)(2,1)} copy(bf16[2,4,128,128]{3,2,1,0:T(8,128)(2,1)S(1)} %shard_map.55) | data formatting | bytes 524288

commit v3 on v2

--- a/solution.py
+++ b/solution.py
@@ -13,9 +13,11 @@
 
 def kernel(
     tiles, slabs, video, w1, b1, w2, b2, out,
-    v, h, k1, k2, bias1, bias2, pieces, incoming, going, going0, sum0, acc,
-    load, w_s, b_s, x_s, z_s, p_s, q_s, o_s, w1_r, b_r, x_r, z_r, p_r, h_r, f_r, q_r, o_r,
+    v, h, k1, k2, bias1, bias2, pieces, incoming, going, going0, sum0, acc, acc2,
+    load, w_s, b_s, z0_s, w1_r, b_r, a_r, z_r, f_r, q_r, o_r,
 ):
+    x_s, p_s, o_s, q_s, z1_s = (load.at[n] for n in range(5))
+    z_s = (z0_s, z1_s)
     frames, rows, columns, channels = video.shape
     half = rows // 2
     width = b2.shape[1]
@@ -95,7 +97,7 @@
     def x_copies(device):
         return [
             [
-                remote(v.at[frames + f, some], v.at[f, some], x_s, x_r.at[2 * f + n], device)
+                remote(v.at[frames + f, some], v.at[f, some], x_s, a_r.at[2 * f + n], device)
                 for n, some in enumerate((low, high))
             ]
             for f in range(BACK)
@@ -105,27 +107,38 @@
     x_in = x_copies(prev_same)
     forward_z = [
         [
-            (above, remote(v.at[f, low], v.at[f, halo_high], z_s.at[0], f_r.at[f], z_minus)),
-            (below, remote(v.at[f, high], v.at[f, halo_low], z_s.at[1], f_r.at[f], z_plus)),
+            (above, remote(v.at[f, low], v.at[f, halo_high], z_s[0], f_r.at[f], z_minus)),
+            (below, remote(v.at[f, high], v.at[f, halo_low], z_s[1], f_r.at[f], z_plus)),
         ]
         for f in range(BACK)
     ]
-    f_in = [remote(v.at[f, low], v.at[f, halo_low], z_s.at[0], f_r.at[f], peer) for f in range(BACK)]
-    forward_p = [remote(v.at[f, low], v.at[f, pl.ds(half, half)], p_s, p_r.at[f], peer) for f in range(BACK)]
-    forward_h = [
-        remote(h.at[BACK + f, low], h.at[BACK + f, pl.ds(half, half)], p_s, h_r.at[f], peer) for f in range(BACK)
+    f_in = [remote(v.at[f, low], v.at[f, halo_low], z_s[0], f_r.at[f], peer) for f in range(BACK)]
+    forward_p = [remote(v.at[f, low], v.at[f, pl.ds(half, half)], p_s, a_r.at[f], peer) for f in range(BACK)]
+
+    def share_h(index, count, place):
+        return remote(
+            h.at[pl.ds(index, count), low], h.at[pl.ds(index, count), pl.ds(half, half)], p_s, a_r.at[2 + place], peer
+        )
+
+    forward_h = [share_h(BACK, 1, 0), share_h(BACK + 1, 1, 1), share_h(frames, 2, 2), share_h(frames, 1, 2)]
+
+    rest_h = [
+        remote(
+            h.at[pl.ds(BACK + n, n + 1), high], h.at[pl.ds(BACK + n, n + 1), pl.ds(rows, half)], o_s, a_r.at[n], peer
+        )
+        for n in range(2)
     ]
 
     def z_copies(count):
         some = pl.ds(BACK, count)
         return [
             [
-                remote(video.at[pl.ds(0, count), pl.ds(n, 1)], v.at[some, pl.ds(rows + n, 1)], z_s.at[0], z_r.at[n], z_minus)
+                remote(video.at[pl.ds(0, count), pl.ds(n, 1)], v.at[some, pl.ds(rows + n, 1)], z_s[0], z_r.at[n], z_minus)
                 for n in range(half)
             ],
             [
                 remote(
-                    v.at[some, pl.ds(rows - 1 - n, 1)], v.at[some, pl.ds(half - 1 - n, 1)], z_s.at[1], z_r.at[n], z_plus
+                    v.at[some, pl.ds(rows - 1 - n, 1)], v.at[some, pl.ds(half - 1 - n, 1)], z_s[1], z_r.at[n], z_plus
                 )
                 for n in range(half)
             ],
@@ -159,13 +172,16 @@
         copy.start()
     with jax.named_scope("loadwait"):
         into_v.wait()
+        own_w1.wait()
+        own_b1.wait()
+        own_b2.wait()
 
     @pl.when(one)
     def _():
         @pl.when(has_next)
         def _():
-            for n in range(2):
-                for f in (1, 0):
+            for f in (1, 0):
+                for n in range(2):
                     x_out[f][n].start()
 
         @pl.when(below)
@@ -199,15 +215,23 @@
     def silu(total):
         return total / (1.0 + jnp.exp(-total))
 
-    def hidden(indices, first, count, oldest=0):
+    def hidden_sum(indices, first, count, steps):
         parts = lax.dot_general(
-            jnp.concatenate([taps(v, index - 2, first, count, range(oldest, 3)) for index in indices], axis=0),
-            jnp.concatenate([k1[tap].reshape(3 * channels, channels) for tap in range(3 * oldest, 9)], axis=1),
+            jnp.concatenate([taps(v, index - 2, first, count, steps) for index in indices], axis=0),
+            jnp.concatenate(
+                [k1[3 * a + b].reshape(3 * channels, channels) for a in steps for b in range(3)], axis=1
+            ),
             (((1,), (1,)), ((), ())),
             preferred_element_type=jnp.float32,
         )
+        return shifted(parts, channels)
+
+    def hidden(indices, first, count, oldest=0, newest=2, before=None):
+        total = hidden_sum(indices, first, count, range(oldest, newest + 1))
+        if before is not None:
+            total = total + before
         bias = jnp.concatenate([bias1[0], bias1[1]], axis=1)
-        value = silu(shifted(parts, channels) + bias).astype(h.dtype)
+        value = silu(total + bias).astype(h.dtype)
         value = value.reshape(len(indices), count, columns, channels)
         for n, index in enumerate(indices):
             h[index, pl.ds(first, count)] = value[n]
@@ -227,19 +251,28 @@
             for index in indices:
                 clear_outside(index)
 
-    def near(*indices):
-        with jax.named_scope("near"):
-            hidden(indices, 1 + core, 1)
-
-    def far(*indices):
-        with jax.named_scope("far"):
+    def near(*indices, oldest=0):
+        with jax.named_scope("near" + "_".join(map(str, indices))):
+            hidden(indices, 1 + core, 1, oldest)
+
+    def far(*indices, oldest=0):
+        with jax.named_scope("far" + "_".join(map(str, indices))):
 
             @pl.when(has_z)
             def _():
-                hidden(indices, (rows - 1) * core, 1)
+                hidden(indices, (rows - 1) * core, 1, oldest)
 
             for index in indices:
                 clear_outside(index)
+
+    def outer_begin(index):
+        with jax.named_scope("outer%da" % index):
+            acc2[...] = hidden_sum((index,), half * core, half, range(1, 3))
+
+    def outer_end(index):
+        with jax.named_scope("outer%db" % index):
+            hidden((index,), half * core, half, 0, 0, acc2[...])
+            clear_outside(index)
 
     def second(index, first, count, steps, blocks):
         matrix = jnp.concatenate(
@@ -283,11 +316,22 @@
             result[t - 1].start()
             out[t, mine] = silu(own + bias2[0]).astype(out.dtype).reshape(half, columns, width)
 
-    def later_steps():
-        with jax.named_scope("latent1a"):
-            halves = second(2, 0, half, range(1, 3), whole)
+    def later_steps(steps=range(1, 3), start=True):
+        with jax.named_scope("latent1a%d" % len(steps)):
+            halves = second(2, 0, half, steps, whole)
             for n in range(2):
-                acc[n] = halves[n]
+                acc[n] = halves[n] if start else acc[n] + halves[n]
+
+    def own_steps(first, ready=None):
+        place = pl.ds(half * core if first == 0 else half, half)
+        with jax.named_scope("own1a"):
+            acc[0] = second(2, first, half, range(1, 3), ((0, 0),))[0]
+        if ready is not None:
+            ready()
+        with jax.named_scope("own"):
+            one_sum, then = second(2, first, half, range(0, 1), ((0, 2), (0, 0)))
+            sum0[place] = one_sum.reshape(half, columns, width)
+            out[1, place] = silu(then + acc[0] + bias2[0]).astype(out.dtype).reshape(half, columns, width)
 
     def last_steps():
         with jax.named_scope("tailA"):
@@ -333,10 +377,6 @@
         with jax.named_scope("w2wait"):
             wait_bytes(k2, load.at[3])
 
-    with jax.named_scope("loadwait"):
-        own_w1.wait()
-        own_b1.wait()
-        own_b2.wait()
     with jax.named_scope("w1wait"):
         remote(w1, k1.at[:, :, other], w_s, w1_r, peer).wait_recv()
         remote(b1, bias1.at[other], b_s.at[0], b_r.at[0], peer).wait_recv()
@@ -344,29 +384,37 @@
 
     last = frames + 1
 
-    @pl.when(has_next)
+    @pl.when(both(one, has_next))
     def _():
         inner(frames, last)
-
-    @pl.when(no_next)
+        forward_h[2].start()
+
+    @pl.when(both(one, no_next))
     def _():
         inner(frames)
-
-    @pl.when(no_prev)
+        forward_h[3].start()
+
+    @pl.when(both(one, no_prev))
     def _():
         inner(3, oldest=1)
+        forward_h[1].start()
         inner(2, oldest=2)
+        forward_h[0].start()
 
     @pl.when(has_next)
     def _():
         wait_z(0, z_full)
         near(frames, last)
         w2_ready()
-
+        from_peer("hwait2", forward_h[2])
         send_share(0, other)
+
         wait_z(1, z_full)
         far(frames, last)
-        send_share(1, core)
+
+        @pl.when(has_prev)
+        def _():
+            send_share(1, core)
 
     def middle():
         for index in range(frames - 1, 3, -1):
@@ -381,44 +429,87 @@
             wait_z(0, z_short)
             wait_z(1, z_short)
             outer(frames)
+
+    def own_ready():
+        @pl.when(no_next)
+        def _():
             w2_ready()
+            from_peer("hwait2", forward_h[3])
 
     @pl.when(no_prev)
     def _():
         own_last()
+        own_ready()
         middle()
+
         outer(3, oldest=1)
-        later_steps()
+
+        @pl.when(one)
+        def _():
+            rest_h[1].start()
+
+        @pl.when(has_next)
+        def _():
+            send_share(1, core)
+
         outer(2, oldest=2)
 
+        @pl.when(one)
+        def _():
+            rest_h[0].start()
+
+        @pl.when(one)
+        def _():
+            own_steps(0)
+
+        @pl.when(zero)
+        def _():
+            forward_h[1].wait_recv()
+            later_steps()
+            forward_h[0].wait_recv()
+            last_steps()
+            with jax.named_scope("rest"):
+                rest_h[1].wait_recv()
+            own_steps(half, rest_h[0].wait_recv)
+
     @pl.when(has_prev)
     def _():
         @pl.when(one)
         def _():
             pass_on(1, 0)
-            pass_on(0, 0)
             pass_on(1, 1)
             inner(3)
             forward_h[1].start()
+            pass_on(0, 0)
+            own_last()
             pass_on(0, 1)
             inner(2)
             forward_h[0].start()
 
-        own_last()
+        @pl.when(zero)
+        def _():
+            own_last()
+
+        own_ready()
         middle()
+        later_steps(range(2, 3))
         from_peer("pwait1", forward_p[1])
         halo_ready("fwait1", f_in[1])
         outer(3)
         from_peer("hwait1", forward_h[1])
-        later_steps()
+        later_steps(range(1, 2), False)
+        outer_begin(2)
         from_peer("pwait0", forward_p[0])
         halo_ready("fwait0", f_in[0])
-        outer(2)
+        outer_end(2)
         from_peer("hwait0", forward_h[0])
-
-    last_steps()
-
-    with jax.named_scope("part0"):
+        last_steps()
+
+
+    takes = jnp.logical_or(has_prev, one)
+
+    @pl.when(takes)
+    def _():
         remote(going0, sum0.at[theirs], o_s, o_r.at[0], peer).wait_recv()
 
     def close(first, count, extra):
@@ -443,7 +534,8 @@
         for copy in to_peer:
             copy.wait_send()
         for t in range(1, frames // 2):
-            remote(going.at[t - 1], out.at[t, theirs], o_s, o_r.at[t], peer).wait_recv()
+            copy = remote(going.at[t - 1], out.at[t, theirs], o_s, o_r.at[t], peer)
+            when(takes if t == 1 else None, copy.wait_recv)
         wait_bytes(v.at[pl.ds(0, frames // 2 + 1), low], o_s)
 
         @pl.when(has_next)
@@ -454,9 +546,14 @@
         def _():
             wait_bytes(v.at[pl.ds(0, BACK), pl.ds(0, rows)], x_s)
 
-        @pl.when(both(one, has_prev))
-        def _():
-            wait_bytes(v.at[pl.ds(0, 2 * BACK), low], p_s)
+        for condition, count in (
+            (both(no_prev, has_next), 4), (both(no_prev, no_next), 3),
+            (both(has_prev, has_next), 6), (both(has_prev, no_next), 5),
+        ):
+
+            @pl.when(both(one, condition))
+            def _():
+                wait_bytes(v.at[pl.ds(0, count), low], p_s)
 
         for side, condition in ((0, above), (1, below)):
             forwards = both(one, condition)
@@ -465,23 +562,23 @@
 
                     @pl.when(both(zero, condition, after))
                     def _():
-                        wait_bytes(v.at[pl.ds(0, count), low], z_s.at[0])
+                        wait_bytes(v.at[pl.ds(0, count), low], z_s[0])
 
                 else:
 
                     @pl.when(both(forwards, after, no_prev))
                     def _():
-                        wait_bytes(v.at[pl.ds(0, count), low], z_s.at[1])
+                        wait_bytes(v.at[pl.ds(0, count), low], z_s[1])
 
                     @pl.when(both(forwards, after, has_prev))
                     def _():
-                        wait_bytes(v.at[pl.ds(0, count + BACK), low], z_s.at[1])
+                        wait_bytes(v.at[pl.ds(0, count + BACK), low], z_s[1])
 
             if side == 0:
 
                 @pl.when(both(forwards, has_prev))
                 def _():
-                    wait_bytes(v.at[pl.ds(0, BACK), low], z_s.at[0])
+                    wait_bytes(v.at[pl.ds(0, BACK), low], z_s[0])
 
 
 def shards(tiles, slabs, video, first_weight, first_bias, second_weight, second_bias):
@@ -502,7 +599,7 @@
         out_specs=inside,
         scratch_shapes=[
             vmem((BACK + frames, rows + 2, columns, channels), jnp.bfloat16),
-            vmem((frames + 2, half + 2, columns, channels), jnp.bfloat16),
+            vmem((frames + 2, half + 4, columns, channels), jnp.bfloat16),
             vmem((9, 3, 2, part, channels), jnp.bfloat16),
             vmem((2, 9, 3, channels, width), jnp.bfloat16),
             vmem((2, 1, part), jnp.float32),
@@ -513,8 +610,9 @@
             vmem((half, columns, width), jnp.float32),
             vmem((rows, columns, width), jnp.float32),
             vmem((2, half * columns, width), jnp.float32),
-            dma((5,)), dma, dma((2,)), dma, dma((2,)), dma, dma, dma, dma, dma((2,)), dma((2 * BACK,)), dma((2,)),
-            dma((BACK,)), dma((BACK,)), dma((BACK,)), dma((2,)), dma((latents,)),
+            vmem((half * columns, channels), jnp.float32),
+            dma((5,)), dma, dma((2,)), dma, dma, dma((2,)), dma((2 * BACK + 1,)), dma((2,)), dma((BACK,)), dma((2,)),
+            dma((latents,)),
         ],
         compiler_params=pltpu.CompilerParams(
             collective_id=0, has_side_effects=True, vmem_limit_bytes=32 << 20

time: 12 us -> 11.5 us (0.958)
  Pallas kernels: 11.2 us -> 10.6 us
    pallas_call x1, Pallas kernels: 11.2 us -> 10.6 us  [shards(): pl.pallas_call(functools.partial(kernel, tiles, slabs), out_shape=jax.Sha...]
where the time goes in v3:
time: 11.5 us; the launch traced here: 11.3 us
  Pallas kernels  10.6 us (92%)
  local copies, waits for them, and re-layouts  0.71 us (6%)
    pallas_call x1, Pallas kernels, shards(): pl.pallas_call(functools.partial(kernel, tiles, slabs), out_shape=jax.Sha...  10.6 us
    unnamed x1, local copies, waits for them, and re-layouts  0.71 us

profile of v3, /device:TPU:19, one launch (start us, length us, event | category | flops | bytes accessed | tf_op | source)
XLA Modules:
  0.0 11.3 jit_solution(11001313034923287602)
XLA Ops:
  0.0 10.6 %shard_map.55 = bf16[2,4,128,128]{3,2,1,0:T(8,128)(2,1)S(1)} custom-call(bf16[4,4,128,128]{3,2,1,0:T(8,128)(2,1)} %video.1, bf16[9,3,64,128]{3,2,1,0:T(8,128)(2,1)} %bitcast.7, f32[1,64]{1,0:T(1,128)} %bitcast.8, bf16[9,3,128,256]{3,2,1,0:T(8,128)(2,1)} %bitcast.6, f32[1,128]{1,0:T(1,128)} %bitcast.9), custom_call_target="tpu_custom_call" | custom-call | tf_op jit(solution)/shard_map/pallas_call | solution.py:595
  10.6 0.7 %copy.7 = bf16[2,4,128,128]{3,2,1,0:T(8,128)(2,1)} copy(bf16[2,4,128,128]{3,2,1,0:T(8,128)(2,1)S(1)} %shard_map.55) | data formatting | bytes 524288

commit v4 on v3

--- a/solution.py
+++ b/solution.py
@@ -57,12 +57,13 @@
         (None, peer),
         (has_z, {"chan": other, "tile": z_tile}),
         (has_prev, {"slab": slab - 1, "chan": 1}),
+        (both(one, has_prev, below), {"slab": slab - 1, "tile": tile + 1, "chan": 1}),
     )
     for condition, device in greetings:
         when(condition, lambda device=device: pl.semaphore_signal(
             barrier, inc=1, device_id=device, device_id_type=MESH))
     met = 1
-    for condition, count in ((has_z, 1), (both(one, has_next), 2)):
+    for condition, count in ((has_z, 1), (both(one, has_next), 2), (both(one, has_next, above), 1)):
         met = met + jnp.where(condition, count, 0)
 
     into_v = pltpu.make_async_copy(video, v.at[pl.ds(BACK, frames), pl.ds(half * other, rows)], load.at[0])
@@ -105,6 +106,7 @@
 
     x_out = x_copies(next_same)
     x_in = x_copies(prev_same)
+    slanted = remote(v.at[frames, low], v.at[0, halo_high], x_s, f_r.at[0], {"slab": slab + 1, **z_minus})
     forward_z = [
         [
             (above, remote(v.at[f, low], v.at[f, halo_high], z_s[0], f_r.at[f], z_minus)),
@@ -226,44 +228,36 @@
         )
         return shifted(parts, channels)
 
-    def hidden(indices, first, count, oldest=0, newest=2, before=None):
+    no_rows = {"inner": (), "near": (), "far": (no_z,), "outer": (both(no_z, zero), both(no_z, one))}
+
+    def hidden(kind, indices, first, count, oldest=0, newest=2, before=None):
         total = hidden_sum(indices, first, count, range(oldest, newest + 1))
         if before is not None:
             total = total + before
         bias = jnp.concatenate([bias1[0], bias1[1]], axis=1)
-        value = silu(total + bias).astype(h.dtype)
+        value = silu(total + bias)
         value = value.reshape(len(indices), count, columns, channels)
         for n, index in enumerate(indices):
-            h[index, pl.ds(first, count)] = value[n]
+            new = value[n]
+            if no_rows[kind]:
+                new = jnp.stack([jnp.where(no_rows[kind][row], 0.0, new[row]) for row in range(count)])
+            h[index, pl.ds(first, count)] = new.astype(h.dtype)
 
     def inner(*indices, oldest=0):
         with jax.named_scope("inner" + "_".join(map(str, indices))):
-            hidden(indices, half * other, half, oldest)
-
-    def clear_outside(index):
-        @pl.when(no_z)
-        def _():
-            h[index, pl.ds((rows - 1) * core, 1)] = jnp.zeros((1, columns, channels), h.dtype)
+            hidden("inner", indices, half * other, half, oldest)
 
     def outer(*indices, oldest=0):
         with jax.named_scope("outer" + "_".join(map(str, indices))):
-            hidden(indices, half * core, half, oldest)
-            for index in indices:
-                clear_outside(index)
+            hidden("outer", indices, half * core, half, oldest)
 
     def near(*indices, oldest=0):
         with jax.named_scope("near" + "_".join(map(str, indices))):
-            hidden(indices, 1 + core, 1, oldest)
+            hidden("near", indices, 1 + core, 1, oldest)
 
     def far(*indices, oldest=0):
         with jax.named_scope("far" + "_".join(map(str, indices))):
-
-            @pl.when(has_z)
-            def _():
-                hidden(indices, (rows - 1) * core, 1, oldest)
-
-            for index in indices:
-                clear_outside(index)
+            hidden("far", indices, (rows - 1) * core, 1, oldest)
 
     def outer_begin(index):
         with jax.named_scope("outer%da" % index):
@@ -271,8 +265,7 @@
 
     def outer_end(index):
         with jax.named_scope("outer%db" % index):
-            hidden((index,), half * core, half, 0, 0, acc2[...])
-            clear_outside(index)
+            hidden("outer", (index,), half * core, half, 0, 0, acc2[...])
 
     def second(index, first, count, steps, blocks):
         matrix = jnp.concatenate(
@@ -322,12 +315,11 @@
             for n in range(2):
                 acc[n] = halves[n] if start else acc[n] + halves[n]
 
-    def own_steps(first, ready=None):
+    def own_steps(first, ready=lambda: None):
         place = pl.ds(half * core if first == 0 else half, half)
         with jax.named_scope("own1a"):
             acc[0] = second(2, first, half, range(1, 3), ((0, 0),))[0]
-        if ready is not None:
-            ready()
+        ready()
         with jax.named_scope("own"):
             one_sum, then = second(2, first, half, range(0, 1), ((0, 2), (0, 0)))
             sum0[place] = one_sum.reshape(half, columns, width)
@@ -356,7 +348,8 @@
         with jax.named_scope("pass%d%d" % (f, n)):
             x_in[f][n].wait_recv()
             condition, copy = forward_z[f][n]
-            pl.when(condition)(copy.start)
+            if (f, n) != (0, 0):
+                pl.when(condition)(copy.start)
             if n == 0:
                 forward_p[f].start()
 
@@ -400,6 +393,10 @@
         forward_h[1].start()
         inner(2, oldest=2)
         forward_h[0].start()
+
+    @pl.when(both(one, has_next, above))
+    def _():
+        slanted.start()
 
     @pl.when(has_next)
     def _():
@@ -410,10 +407,10 @@
         send_share(0, other)
 
         wait_z(1, z_full)
-        far(frames, last)
-
-        @pl.when(has_prev)
-        def _():
+
+        @pl.when(jnp.logical_or(above, has_prev))
+        def _():
+            far(frames, last)
             send_share(1, core)
 
     def middle():
@@ -442,34 +439,37 @@
         own_ready()
         middle()
 
-        outer(3, oldest=1)
+        @pl.when(both(has_next, tile == 0))
+        def _():
+            far(frames, last)
+            outer(3, oldest=1)
+            outer(2, oldest=2)
+
+        @pl.when(jnp.logical_or(above, no_next))
+        def _():
+            outer(3, oldest=1)
+            outer(2, oldest=2)
 
         @pl.when(one)
         def _():
             rest_h[1].start()
-
-        @pl.when(has_next)
+            rest_h[0].start()
+
+        @pl.when(both(has_next, tile == 0))
         def _():
             send_share(1, core)
 
-        outer(2, oldest=2)
-
         @pl.when(one)
         def _():
-            rest_h[0].start()
-
-        @pl.when(one)
-        def _():
             own_steps(0)
 
         @pl.when(zero)
         def _():
             forward_h[1].wait_recv()
+            forward_h[0].wait_recv()
             later_steps()
-            forward_h[0].wait_recv()
             last_steps()
-            with jax.named_scope("rest"):
-                rest_h[1].wait_recv()
+            rest_h[1].wait_recv()
             own_steps(half, rest_h[0].wait_recv)
 
     @pl.when(has_prev)
@@ -495,14 +495,14 @@
         later_steps(range(2, 3))
         from_peer("pwait1", forward_p[1])
         halo_ready("fwait1", f_in[1])
+        from_peer("hwait1", forward_h[1])
         outer(3)
-        from_peer("hwait1", forward_h[1])
         later_steps(range(1, 2), False)
         outer_begin(2)
         from_peer("pwait0", forward_p[0])
+        from_peer("hwait0", forward_h[0])
         halo_ready("fwait0", f_in[0])
         outer_end(2)
-        from_peer("hwait0", forward_h[0])
         last_steps()
 
 
@@ -542,9 +542,13 @@
         def _():
             wait_bytes(incoming, q_s)
 
-        @pl.when(both(one, has_next))
+        @pl.when(both(one, has_next, tile == 0))
         def _():
             wait_bytes(v.at[pl.ds(0, BACK), pl.ds(0, rows)], x_s)
+
+        @pl.when(both(one, has_next, above))
+        def _():
+            wait_bytes(v.at[pl.ds(0, BACK), pl.ds(0, rows + 1)], x_s)
 
         for condition, count in (
             (both(no_prev, has_next), 4), (both(no_prev, no_next), 3),
@@ -578,7 +582,7 @@
 
                 @pl.when(both(forwards, has_prev))
                 def _():
-                    wait_bytes(v.at[pl.ds(0, BACK), low], z_s[0])
+                    wait_bytes(v.at[pl.ds(0, 1), low], z_s[0])
 
 
 def shards(tiles, slabs, video, first_weight, first_bias, second_weight, second_bias):

time: 11.5 us -> 11.4 us (level)
  no operation moved by 1% of the time
where the time goes in v4:
time: 11.4 us; the launch traced here: 11.3 us
  Pallas kernels  10.6 us (93%)
  local copies, waits for them, and re-layouts  0.71 us (6%)
    pallas_call x1, Pallas kernels, shards(): pl.pallas_call(functools.partial(kernel, tiles, slabs), out_shape=jax.Sha...  10.6 us
    unnamed x1, local copies, waits for them, and re-layouts  0.71 us

profile of v4, /device:TPU:19, one launch (start us, length us, event | category | flops | bytes accessed | tf_op | source)
XLA Modules:
  0.0 11.3 jit_solution(461122069850163744)
XLA Ops:
  0.0 10.6 %shard_map.55 = bf16[2,4,128,128]{3,2,1,0:T(8,128)(2,1)S(1)} custom-call(bf16[4,4,128,128]{3,2,1,0:T(8,128)(2,1)} %video.1, bf16[9,3,64,128]{3,2,1,0:T(8,128)(2,1)} %bitcast.7, f32[1,64]{1,0:T(1,128)} %bitcast.8, bf16[9,3,128,256]{3,2,1,0:T(8,128)(2,1)} %bitcast.6, f32[1,128]{1,0:T(1,128)} %bitcast.9), custom_call_target="tpu_custom_call" | custom-call | tf_op jit(solution)/shard_map/pallas_call | solution.py:599
  10.6 0.7 %copy.7 = bf16[2,4,128,128]{3,2,1,0:T(8,128)(2,1)} copy(bf16[2,4,128,128]{3,2,1,0:T(8,128)(2,1)S(1)} %shard_map.55) | data formatting | bytes 524288

commit v5 on v4

--- a/solution.py
+++ b/solution.py
@@ -182,9 +182,8 @@
     def _():
         @pl.when(has_next)
         def _():
-            for f in (1, 0):
-                for n in range(2):
-                    x_out[f][n].start()
+            for f, n in ((1, 0), (1, 1), (0, 1), (0, 0)):
+                x_out[f][n].start()
 
         @pl.when(below)
         def _():
@@ -315,11 +314,10 @@
             for n in range(2):
                 acc[n] = halves[n] if start else acc[n] + halves[n]
 
-    def own_steps(first, ready=lambda: None):
+    def own_steps(first):
         place = pl.ds(half * core if first == 0 else half, half)
         with jax.named_scope("own1a"):
             acc[0] = second(2, first, half, range(1, 3), ((0, 0),))[0]
-        ready()
         with jax.named_scope("own"):
             one_sum, then = second(2, first, half, range(0, 1), ((0, 2), (0, 0)))
             sum0[place] = one_sum.reshape(half, columns, width)
@@ -469,8 +467,9 @@
             forward_h[0].wait_recv()
             later_steps()
             last_steps()
-            rest_h[1].wait_recv()
-            own_steps(half, rest_h[0].wait_recv)
+            for copy in rest_h:
+                copy.wait_recv()
+            own_steps(half)
 
     @pl.when(has_prev)
     def _():
@@ -480,9 +479,9 @@
             pass_on(1, 1)
             inner(3)
             forward_h[1].start()
+            pass_on(0, 1)
+            own_last()
             pass_on(0, 0)
-            own_last()
-            pass_on(0, 1)
             inner(2)
             forward_h[0].start()
 

time: 11.4 us -> 11.3 us (level)
  no operation moved by 1% of the time
where the time goes in v5:
time: 11.3 us; the launch traced here: 11.2 us
  Pallas kernels  10.5 us (93%)
  local copies, waits for them, and re-layouts  0.71 us (6%)
    pallas_call x1, Pallas kernels, shards(): pl.pallas_call(functools.partial(kernel, tiles, slabs), out_shape=jax.Sha...  10.5 us
    unnamed x1, local copies, waits for them, and re-layouts  0.71 us

profile of v5, /device:TPU:19, one launch (start us, length us, event | category | flops | bytes accessed | tf_op | source)
XLA Modules:
  0.0 11.2 jit_solution(4106336217837477290)
XLA Ops:
  0.0 10.5 %shard_map.55 = bf16[2,4,128,128]{3,2,1,0:T(8,128)(2,1)S(1)} custom-call(bf16[4,4,128,128]{3,2,1,0:T(8,128)(2,1)} %video.1, bf16[9,3,64,128]{3,2,1,0:T(8,128)(2,1)} %bitcast.7, f32[1,64]{1,0:T(1,128)} %bitcast.8, bf16[9,3,128,256]{3,2,1,0:T(8,128)(2,1)} %bitcast.6, f32[1,128]{1,0:T(1,128)} %bitcast.9), custom_call_target="tpu_custom_call" | custom-call | tf_op jit(solution)/shard_map/pallas_call | solution.py:598
  10.5 0.7 %copy.7 = bf16[2,4,128,128]{3,2,1,0:T(8,128)(2,1)} copy(bf16[2,4,128,128]{3,2,1,0:T(8,128)(2,1)S(1)} %shard_map.55) | data formatting | bytes 524288

commit v6 on v5

--- a/solution.py
+++ b/solution.py
@@ -492,17 +492,28 @@
         own_ready()
         middle()
         later_steps(range(2, 3))
-        from_peer("pwait1", forward_p[1])
-        halo_ready("fwait1", f_in[1])
-        from_peer("hwait1", forward_h[1])
-        outer(3)
-        later_steps(range(1, 2), False)
-        outer_begin(2)
-        from_peer("pwait0", forward_p[0])
-        from_peer("hwait0", forward_h[0])
-        halo_ready("fwait0", f_in[0])
-        outer_end(2)
-        last_steps()
+        @pl.when(one)
+        def _():
+            halo_ready("fwait1", f_in[1])
+            halo_ready("fwait0", f_in[0])
+            outer(3)
+            outer(2)
+            later_steps(range(1, 2), False)
+            last_steps()
+
+        @pl.when(zero)
+        def _():
+            forward_p[1].wait_recv()
+            halo_ready("fwait1", f_in[1])
+            forward_h[1].wait_recv()
+            outer(3)
+            later_steps(range(1, 2), False)
+            outer_begin(2)
+            forward_p[0].wait_recv()
+            forward_h[0].wait_recv()
+            halo_ready("fwait0", f_in[0])
+            outer_end(2)
+            last_steps()
 
 
     takes = jnp.logical_or(has_prev, one)

time: 11.3 us -> 11.3 us (level)
  no operation moved by 1% of the time
where the time goes in v6:
time: 11.3 us; the launch traced here: 11.2 us
  Pallas kernels  10.5 us (93%)
  local copies, waits for them, and re-layouts  0.71 us (6%)
    pallas_call x1, Pallas kernels, shards(): pl.pallas_call(functools.partial(kernel, tiles, slabs), out_shape=jax.Sha...  10.5 us
    unnamed x1, local copies, waits for them, and re-layouts  0.71 us

profile of v6, /device:TPU:19, one launch (start us, length us, event | category | flops | bytes accessed | tf_op | source)
XLA Modules:
  0.0 11.2 jit_solution(527879967479191116)
XLA Ops:
  0.0 10.5 %shard_map.55 = bf16[2,4,128,128]{3,2,1,0:T(8,128)(2,1)S(1)} custom-call(bf16[4,4,128,128]{3,2,1,0:T(8,128)(2,1)} %video.1, bf16[9,3,64,128]{3,2,1,0:T(8,128)(2,1)} %bitcast.7, f32[1,64]{1,0:T(1,128)} %bitcast.8, bf16[9,3,128,256]{3,2,1,0:T(8,128)(2,1)} %bitcast.6, f32[1,128]{1,0:T(1,128)} %bitcast.9), custom_call_target="tpu_custom_call" | custom-call | tf_op jit(solution)/shard_map/pallas_call | solution.py:609
  10.5 0.7 %copy.7 = bf16[2,4,128,128]{3,2,1,0:T(8,128)(2,1)} copy(bf16[2,4,128,128]{3,2,1,0:T(8,128)(2,1)S(1)} %shard_map.55) | data formatting | bytes 524288

commit v7 on v6

--- a/solution.py
+++ b/solution.py
@@ -294,7 +294,13 @@
             halves = second(frames, local, 1, range(0, 2), whole)
             for n in (1, 0):
                 pieces[slot, n] = halves[n].astype(pieces.dtype)
-                shares[slot][n].start()
+            for condition, order in ((zero, (0, 1)), (one, (1, 0))):
+
+                @pl.when(condition)
+                def _():
+                    for n in order:
+                        shares[slot][n].start()
+
 
     result = [
         remote(going.at[t - 1], out.at[t, mine], o_s, o_r.at[t], peer) for t in range(1, frames // 2)

time: 11.3 us -> 11.2 us (level)
  Pallas kernels: 10.5 us -> 10.3 us
    pallas_call x1, Pallas kernels: 10.5 us -> 10.3 us  [shards(): pl.pallas_call(functools.partial(kernel, tiles, slabs), out_shape=jax.Sha...]
where the time goes in v7:
time: 11.2 us; the launch traced here: 11.1 us
  Pallas kernels  10.3 us (92%)
  local copies, waits for them, and re-layouts  0.71 us (6%)
    pallas_call x1, Pallas kernels, shards(): pl.pallas_call(functools.partial(kernel, tiles, slabs), out_shape=jax.Sha...  10.3 us
    unnamed x1, local copies, waits for them, and re-layouts  0.71 us

profile of v7, /device:TPU:19, one launch (start us, length us, event | category | flops | bytes accessed | tf_op | source)
XLA Modules:
  0.0 11.1 jit_solution(427673512863511232)
XLA Ops:
  0.0 10.3 %shard_map.55 = bf16[2,4,128,128]{3,2,1,0:T(8,128)(2,1)S(1)} custom-call(bf16[4,4,128,128]{3,2,1,0:T(8,128)(2,1)} %video.1, bf16[9,3,64,128]{3,2,1,0:T(8,128)(2,1)} %bitcast.7, f32[1,64]{1,0:T(1,128)} %bitcast.8, bf16[9,3,128,256]{3,2,1,0:T(8,128)(2,1)} %bitcast.6, f32[1,128]{1,0:T(1,128)} %bitcast.9), custom_call_target="tpu_custom_call" | custom-call | tf_op jit(solution)/shard_map/pallas_call | solution.py:615
  10.4 0.7 %copy.7 = bf16[2,4,128,128]{3,2,1,0:T(8,128)(2,1)} copy(bf16[2,4,128,128]{3,2,1,0:T(8,128)(2,1)S(1)} %shard_map.55) | data formatting | bytes 524288

commit v8 on v7

--- a/solution.py
+++ b/solution.py
@@ -511,14 +511,13 @@
         def _():
             forward_p[1].wait_recv()
             halo_ready("fwait1", f_in[1])
+            outer(3)
             forward_h[1].wait_recv()
-            outer(3)
-            later_steps(range(1, 2), False)
-            outer_begin(2)
             forward_p[0].wait_recv()
             forward_h[0].wait_recv()
             halo_ready("fwait0", f_in[0])
-            outer_end(2)
+            outer(2)
+            later_steps(range(1, 2), False)
             last_steps()
 
 

time: 11.2 us -> 11.2 us (level)
  no operation moved by 1% of the time
where the time goes in v8:
time: 11.2 us; the launch traced here: 11.1 us
  Pallas kernels  10.3 us (92%)
  local copies, waits for them, and re-layouts  0.71 us (6%)
    pallas_call x1, Pallas kernels, shards(): pl.pallas_call(functools.partial(kernel, tiles, slabs), out_shape=jax.Sha...  10.3 us
    unnamed x1, local copies, waits for them, and re-layouts  0.71 us

profile of v8, /device:TPU:19, one launch (start us, length us, event | category | flops | bytes accessed | tf_op | source)
XLA Modules:
  0.0 11.1 jit_solution(16197599107275555223)
XLA Ops:
  0.0 10.3 %shard_map.55 = bf16[2,4,128,128]{3,2,1,0:T(8,128)(2,1)S(1)} custom-call(bf16[4,4,128,128]{3,2,1,0:T(8,128)(2,1)} %video.1, bf16[9,3,64,128]{3,2,1,0:T(8,128)(2,1)} %bitcast.7, f32[1,64]{1,0:T(1,128)} %bitcast.8, bf16[9,3,128,256]{3,2,1,0:T(8,128)(2,1)} %bitcast.6, f32[1,128]{1,0:T(1,128)} %bitcast.9), custom_call_target="tpu_custom_call" | custom-call | tf_op jit(solution)/shard_map/pallas_call | solution.py:614
  10.4 0.7 %copy.7 = bf16[2,4,128,128]{3,2,1,0:T(8,128)(2,1)} copy(bf16[2,4,128,128]{3,2,1,0:T(8,128)(2,1)S(1)} %shard_map.55) | data formatting | bytes 524288

commit v9 on v8

--- a/solution.py
+++ b/solution.py
@@ -404,10 +404,10 @@
 
     @pl.when(has_next)
     def _():
+        w2_ready()
+        from_peer("hwait2", forward_h[2])
         wait_z(0, z_full)
         near(frames, last)
-        w2_ready()
-        from_peer("hwait2", forward_h[2])
         send_share(0, other)
 
         wait_z(1, z_full)

time: 11.2 us -> 11.2 us (level)
  no operation moved by 1% of the time
where the time goes in v9:
time: 11.2 us; the launch traced here: 11 us
  Pallas kernels  10.3 us (92%)
  local copies, waits for them, and re-layouts  0.71 us (6%)
    pallas_call x1, Pallas kernels, shards(): pl.pallas_call(functools.partial(kernel, tiles, slabs), out_shape=jax.Sha...  10.3 us
    unnamed x1, local copies, waits for them, and re-layouts  0.71 us

profile of v9, /device:TPU:19, one launch (start us, length us, event | category | flops | bytes accessed | tf_op | source)
XLA Modules:
  0.0 11.0 jit_solution(12534385898224756472)
XLA Ops:
  0.0 10.3 %shard_map.55 = bf16[2,4,128,128]{3,2,1,0:T(8,128)(2,1)S(1)} custom-call(bf16[4,4,128,128]{3,2,1,0:T(8,128)(2,1)} %video.1, bf16[9,3,64,128]{3,2,1,0:T(8,128)(2,1)} %bitcast.7, f32[1,64]{1,0:T(1,128)} %bitcast.8, bf16[9,3,128,256]{3,2,1,0:T(8,128)(2,1)} %bitcast.6, f32[1,128]{1,0:T(1,128)} %bitcast.9), custom_call_target="tpu_custom_call" | custom-call | tf_op jit(solution)/shard_map/pallas_call | solution.py:614
  10.3 0.7 %copy.7 = bf16[2,4,128,128]{3,2,1,0:T(8,128)(2,1)} copy(bf16[2,4,128,128]{3,2,1,0:T(8,128)(2,1)S(1)} %shard_map.55) | data formatting | bytes 524288
